TPU v7x, 32 devices: a whole 2x2x4 slice. The times are simulated.
32 devices in a mesh: half: 2 (over x), seq: 4 (over z), head: 4 (over y, core).
Axes of the slice: x: 2, y: 2, z: 4, core: 2. Of those that a mesh axis runs over, the one named last changes fastest.
Arguments:
- enc_states: bfloat16 [8192, 4096], P(('half', 'seq')), may hold values from -64 to 64
- norm_gain: float32 [4096], replicated, may hold values from 0.25 to 4
- kv_weight: bfloat16 [4096, 1024], P(None, 'head'), may hold values from -1 to 1
- queries: bfloat16 [1024, 4096], P(('half', 'seq'), 'head'), may hold values from -512 to 512
- cotangent: bfloat16 [1024, 4096], P(('half', 'seq'), 'head'), may hold values from -8 to 8
Outputs:
- context: bfloat16 [1024, 4096], P(('half', 'seq'), 'head')
- d_queries: bfloat16 [1024, 4096], P(('half', 'seq'), 'head')
- d_keys_values: bfloat16 [8192, 1024], P(('half', 'seq'), 'head')
All inputs are finite; a program needn't handle non-finite values.
Results may differ from a plain program's by a relative error of at most 0.013.
The roundings to bfloat16 on the way count: a program that leaves them out, or rounds other values in their place, can miss the bound.
Values may be sent and summed in bfloat16 or wider, within the bound.
No kernel may reach another device: no remote copies, remote signals or barrier semaphores. Data moves between devices by JAX's collectives and lax.ppermute only.
A program may use at most 128 MiB of HBM per device.

v0:
```python
import jax
import jax.numpy as jnp
from jax import lax
from jax.sharding import PartitionSpec as P

HD = 64
eps = 1e-06
block_rows = 1024


def block_of():
    return block_rows


def split_blocks(tensor):
    block_size = block_of()
    return tensor.reshape((tensor.shape[0] // block_size, block_size) + tensor.shape[1:])


def join_blocks(tensor):
    return tensor.reshape((tensor.shape[0] * tensor.shape[1],) + tensor.shape[2:])


def to_rows(matrix, groups, head_size):
    tokens = matrix.shape[0]
    per_group = matrix.shape[1] // (groups * head_size)
    shaped = matrix.reshape(tokens, groups, per_group, head_size).transpose(0, 2, 1, 3)
    return shaped.reshape(tokens * per_group, groups, head_size)


def from_rows(row_tensor, tokens):
    length, groups, head_size = row_tensor.shape
    per_group = length // tokens
    shaped = row_tensor.reshape(tokens, per_group, groups, head_size).transpose(0, 2, 1, 3)
    return shaped.reshape(tokens, groups * per_group * head_size)


def block_scores(query_block, pair_block, head_size):
    length = pair_block.shape[0]
    pieces = pair_block.reshape(length, -1, 2, head_size)
    key_rows = pieces[:, :, 0, :]
    values = pieces[:, :, 1, :]
    scores = jnp.einsum("rgd,bgd->rgb", query_block, key_rows, preferred_element_type=jnp.float32)
    return (scores * head_size ** (-0.5), key_rows, values)


def row_maxima(query_rows, pair_rows, head_size):

    def row_by_rows(query_block):

        def row_advance(largest, pair_block):
            scores = block_scores(query_block, pair_block, head_size)[0]
            return (jnp.maximum(largest, jnp.max(scores, axis=2)), None)

        initial = jnp.full(query_block.shape[:2], -jnp.inf, jnp.float32)
        return lax.scan(row_advance, initial, split_blocks(pair_rows))[0]

    return join_blocks(lax.map(row_by_rows, split_blocks(query_rows)))


def weighted_sums(query_rows, pair_rows, row_max, head_size):

    def weighted_by_rows(blocks):
        query_block, max_block = blocks

        def weighted_advance(running, pair_block):
            totals, accumulated = running
            scores, key_rows, values = block_scores(query_block, pair_block, head_size)
            exponent = jnp.exp(scores - max_block[:, :, None])
            accumulated = accumulated + jnp.einsum(
                "rgb,bgd->rgd",
                exponent.astype(jnp.bfloat16),
                values,
                preferred_element_type=jnp.float32,
            )
            return ((totals + jnp.sum(exponent, axis=2), accumulated), None)

        initial = (
            jnp.zeros(max_block.shape, jnp.float32),
            jnp.zeros(query_block.shape, jnp.float32),
        )
        return lax.scan(weighted_advance, initial, split_blocks(pair_rows))[0]

    totals, accumulated = lax.map(
        weighted_by_rows, (split_blocks(query_rows), split_blocks(row_max))
    )
    return (join_blocks(totals), join_blocks(accumulated))


def gradients(query_rows, grad_rows, pair_rows, row_max, totals, deltas, head_size):
    pair_blocks = split_blocks(pair_rows)

    def gradients_by_rows(pair_sum, blocks):
        query_block, grad_block, max_block, total_block, delta_block = blocks

        def gradients_advance(query_sum, pair_block):
            scores, key_rows, values = block_scores(query_block, pair_block, head_size)
            probability = jnp.exp(scores - max_block[:, :, None]) / total_block[:, :, None]
            prob_grad = jnp.einsum(
                "rgd,bgd->rgb", grad_block, values, preferred_element_type=jnp.float32
            )
            score_grad = (
                head_size ** (-0.5) * probability * (prob_grad - delta_block[:, :, None])
            ).astype(jnp.bfloat16)
            query_sum = query_sum + jnp.einsum(
                "rgb,bgd->rgd", score_grad, key_rows, preferred_element_type=jnp.float32
            )
            key_grad = jnp.einsum(
                "rgb,rgd->bgd", score_grad, query_block, preferred_element_type=jnp.float32
            )
            value_grad = jnp.einsum(
                "rgb,rgd->bgd",
                probability.astype(jnp.bfloat16),
                grad_block,
                preferred_element_type=jnp.float32,
            )
            return (
                query_sum,
                jnp.stack([key_grad, value_grad], axis=2).reshape(pair_block.shape[0], -1),
            )

        query_grad, pair_parts = lax.scan(
            gradients_advance, jnp.zeros(query_block.shape, jnp.float32), pair_blocks
        )
        return (pair_sum + pair_parts, query_grad)

    initial = jnp.zeros(pair_blocks.shape, jnp.float32)
    blocks = (
        split_blocks(query_rows),
        split_blocks(grad_rows),
        split_blocks(row_max),
        split_blocks(totals),
        split_blocks(deltas),
    )
    pair_grad, query_grad = lax.scan(gradients_by_rows, initial, blocks)
    return (join_blocks(query_grad), join_blocks(pair_grad))


def on_device(enc_states, norm_gain, kv_weight, queries, cotangent):
    groups = kv_weight.shape[1] // (2 * HD)
    states = enc_states.astype(jnp.float32)
    inverse_root = lax.rsqrt(jnp.mean(states * states, axis=1, keepdims=True) + eps)
    normed = (states * inverse_root * norm_gain).astype(jnp.bfloat16)
    own_pairs = jnp.dot(normed, kv_weight, preferred_element_type=jnp.float32).astype(jnp.bfloat16)
    tokens = queries.shape[0]
    query_rows = to_rows(queries, groups, HD)
    grad_rows = to_rows(cotangent, groups, HD)
    fragment = lax.all_gather(own_pairs, ("half", "seq"), axis=0, tiled=True)
    row_max = row_maxima(query_rows, fragment, HD)
    totals, accumulated = weighted_sums(query_rows, fragment, row_max, HD)
    context_rows = (accumulated / totals[:, :, None]).astype(jnp.bfloat16)
    deltas = jnp.sum(grad_rows.astype(jnp.float32) * context_rows.astype(jnp.float32), axis=2)
    query_grad, pair_grad = gradients(query_rows, grad_rows, fragment, row_max, totals, deltas, HD)
    pair_share = lax.psum_scatter(pair_grad, ("half", "seq"), scatter_dimension=0, tiled=True)
    context = from_rows(context_rows, tokens)
    d_queries = from_rows(query_grad.astype(jnp.bfloat16), tokens)
    return (context, d_queries, pair_share.astype(jnp.bfloat16))


def solution(mesh):
    placed = (
        P(("half", "seq"), None),
        P(),
        P(None, "head"),
        P(("half", "seq"), "head"),
        P(("half", "seq"), "head"),
    )
    return jax.shard_map(
        on_device,
        mesh=mesh,
        in_specs=placed,
        out_specs=(
            P(("half", "seq"), "head"),
            P(("half", "seq"), "head"),
            P(("half", "seq"), "head"),
        ),
        check_vma=False,
    )
```

profile of v0, /device:TPU:0, one launch (start us, length us, event | category | flops | bytes accessed | tf_op | source)
XLA Modules:
  0.0 438.9 jit_solution(8884652493314864029)
XLA Ops:
  7.2 5.2 %fusion.23 = f32[1024]{0:T(1024)S(1)} fusion(bf16[1024,4096]{1,0:T(8,128)(2,1)} %param.11), kind=kLoop, calls=%fused_computation.36 | loop fusion | flops 12581888 | bytes 8392704 | tf_op jit(solution)/shard_map/reduce_sum | solution.py:142
  13.6 4.0 fusion.30
  18.6 1.8 copy.35
  22.6 70.7 %all-gather.2.cloned.1.call-done = bf16[8192,256]{1,0:T(8,128)(2,1)} async-done(((bf16[1024,256]{1,0:T(8,128)(2,1)}), bf16[8192,256]{1,0:T(8,128)(2,1)}) %all-gather.2.cloned.1.call-update) | async-done | bytes 4194320 | tf_op jit(solution)/shard_map/all_gather | solution.py:148
  93.3 6.5 %copy.31 = bf16[8,1024,256]{1,2,0:T(8,128)(2,1)} copy(bf16[8,1024,256]{2,1,0:T(8,128)(2,1)} %bitcast.177) | data formatting | bytes 8388608
  99.8 19.5 %while.62 = (s32[]{:T(128)}, f32[1024,2]{0,1:T(2,128)S(1)}, bf16[8,1024,256]{1,2,0:T(8,128)(2,1)}, bf16[1024,2,64]{0,2,1:T(8,128)(2,1)S(1)}, s32[]{:T(128)}, /*index=5*/s32[]{:T(128)}) while((s32[]{:T(128)}, f32[1024,2]{0,1:T(2,128)S(1)}, bf16[8,1024,256]{1,2,0:T(8,128)(2,1)}, bf16[1024,2,64]{0,2,1:T(8,128)(2,1)S(1)}, s32[]{:T(128)}, ...), condition=%wide.region_3.0_spmd.clone, body=%wide.region_1.3_spmd.clone.sunk | while | flops 272631808 | bytes 1605723 | solution.py:56
  119.3 36.3 %while.63 = (s32[]{:T(128)}, f32[1024,2]{0,1:T(2,128)S(1)}, f32[1024,2,64]{0,2,1:T(8,128)S(1)}, bf16[8,1024,256]{1,2,0:T(8,128)(2,1)}, bf16[1024,2,64]{0,2,1:T(8...) while((s32[]{:T(128)}, f32[1024,2]{0,1:T(2,128)S(1)}, ...), condition=%wide.region_6.7_spmd.clone, body=%wide.region_4.0_spmd.clone.sunk | while | flops 549718016 | bytes 19710060 | solution.py:82
  120.4 1.8 fusion.63
  122.2 1.6 fusion.64
  124.9 1.8 fusion.63
  126.7 1.6 fusion.64
  129.5 1.8 fusion.63
  131.2 1.6 fusion.64
  134.0 1.8 fusion.63
  135.8 1.6 fusion.64
  138.5 1.8 fusion.63
  140.3 1.6 fusion.64
  143.1 1.8 fusion.63
  144.9 1.6 fusion.64
  147.6 1.8 fusion.63
  149.4 1.6 fusion.64
  152.1 1.8 fusion.63
  153.9 1.6 fusion.64
  157.1 2.6 multiply_reduce_fusion.1
  159.8 124.0 %while.64 = (s32[]{:T(128)}, f32[1024,2,64]{0,2,1:T(8,128)}, f32[8,1024,256]{2,1,0:T(8,128)}, bf16[8,1024,256]{1,2,0:T(8,128)(2,1)}, bf16[1024,2,64]{0,2,1:T(8,1...) while((s32[]{:T(128)}, f32[1024,2,64]{0,2,1:T(8,128)}, ...), condition=%wide.region_9.10_spmd.clone, body=%wide.region_8.9_spmd.clone.sunk | while | flops 1359478784 | bytes 51142788 | solution.py:122
  160.9 1.9 fusion.72
  162.8 2.3 fusion.75
  165.1 2.3 fusion.73
  167.4 1.7 fusion.74
  171.7 1.6 copy.61
  175.4 1.9 fusion.72
  177.4 2.3 fusion.75
  179.7 2.3 fusion.73
  182.0 2.7 fusion.74
  187.3 1.6 copy.61
  191.1 1.9 fusion.72
  193.0 2.3 fusion.75
  195.4 2.3 fusion.73
  197.6 2.7 fusion.74
  203.0 1.6 copy.61
  206.7 1.9 fusion.72
  208.6 2.3 fusion.75
  211.0 2.3 fusion.73
  213.3 2.7 fusion.74
  218.6 1.6 copy.61
  222.3 1.9 fusion.72
  224.2 2.3 fusion.75
  226.6 2.3 fusion.73
  228.9 2.7 fusion.74
  237.9 1.9 fusion.72
  239.8 2.3 fusion.75
  242.2 2.3 fusion.73
  244.5 2.7 fusion.74
  249.8 1.6 copy.61
  253.6 1.9 fusion.72
  255.5 2.3 fusion.75
  257.8 2.3 fusion.73
  260.1 2.7 fusion.74
  269.2 1.9 fusion.72
  271.1 2.3 fusion.75
  273.5 2.3 fusion.73
  275.7 2.7 fusion.74
  288.5 141.5 %reduce-scatter.2.cloned.1.call-done = f32[1024,256]{1,0:T(8,128)} async-done(((f32[8192,256]{1,0:T(8,128)}), f32[1024,256]{1,0:T(8,128)}) %reduce-scatter.2.cloned.1.call-update) | async-done | bytes 1048592 | tf_op jit(solution)/shard_map/reduce_scatter | solution.py:154
  430.0 2.1 convert_element_type.49
  (115 shorter events, 81.7 us)
Async XLA Ops:
  7.2 5.3 %copy-start = (bf16[4096,256]{1,0:T(8,128)(2,1)S(1)}, bf16[4096,256]{1,0:T(8,128)(2,1)}, u32[]{:S(2)}) copy-start(bf16[4096,256]{1,0:T(8,128)(2,1)} %param.13) | copy-start | bytes 6291460
  7.2 86.1 %all-gather.2.cloned.1.call-start = ((), (), s32[]{:S(2)}) async-start(), calls=%async_computation.1 | async-start | bytes 4718592 | tf_op jit(solution)/shard_map/all_gather | solution.py:148
  7.2 6.4 %copy-start.1 = (bf16[1024,4096]{1,0:T(8,128)(2,1)S(1)}, bf16[1024,4096]{1,0:T(8,128)(2,1)}, u32[]{:S(2)}) copy-start(bf16[1024,4096]{1,0:T(8,128)(2,1)} %param.11) | copy-start | bytes 25165828
  13.6 4.3 copy-start.3
  17.6 412.3 %reduce-scatter.2.cloned.1.call-start = ((), (), s32[]{:S(2)}) async-start(), calls=%async_computation.2 | async-start | bytes 9437184 | tf_op jit(solution)/shard_map/reduce_scatter | solution.py:154
  283.7 1.0 copy-start.2
Sparse Core Ops, SparseCore 0:
  17.8 75.4 all-gather.1
  283.9 146.0 reduce-scatter.1
where the time goes:
time: 442 us; the launch traced here: 439 us
  waiting for transfers between devices  212 us (48%)
  matrix products  126 us (29%)
  local copies, waits for them, and re-layouts  73.6 us (17%)
  between operations  14.2 us (3%)
  other arithmetic  12 us (3%)
    reduce_scatter x1, waiting for transfers between devices, on_device(): lax.psum_scatter(pair_grad, ('half', 'seq'), scatter_dimension=0, tiled=T...  141 us
    all_gather x1, waiting for transfers between devices, on_device(): fragment = lax.all_gather(own_pairs, ('half', 'seq'), axis=0, tiled=True)  70.7 us
    dot_general x24, matrix products, block_scores(): jnp.einsum('rgd,bgd->rgb', query_block, key_rows, preferred_element_type=...  40 us
    dynamic_slice x24, local copies, waits for them, and re-layouts, row_by_rows(): return lax.scan(row_advance, initial, split_blocks(pair_rows))[0]  25.9 us
    dynamic_update_slice x16, local copies, waits for them, and re-layouts, gradients_by_rows(): lax.scan(gradients_advance, jnp.zeros(query_block.shape, jnp.float32), pa...  21 us
    dot_general x8, matrix products, gradients_advance(): jnp.einsum('rgb,bgd->rgd', score_grad, key_rows, preferred_element_type=j...  20.5 us
    dot_general x8, matrix products, gradients_advance(): jnp.einsum('rgb,rgd->bgd', probability.astype(jnp.bfloat16), grad_block,...  18.8 us
    dot_general x8, matrix products, gradients_advance(): jnp.einsum('rgd,bgd->rgb', grad_block, values, preferred_element_type=jnp...  18.3 us
  transfers between devices with their start and end apart: 2, of which 2 were waited for; matrix products, arithmetic and copies ran while one was open for 2% of the time, Pallas kernels for 0%

commit v1 on v0

--- a/solution.py
+++ b/solution.py
@@ -145,7 +145,13 @@
     tokens = queries.shape[0]
     query_rows = to_rows(queries, groups, HD)
     grad_rows = to_rows(cotangent, groups, HD)
-    fragment = lax.all_gather(own_pairs, ("half", "seq"), axis=0, tiled=True)
+    map_object_by_axis = lambda dim_k, in_array: jnp.concatenate(
+        lax.all_to_all(
+            jnp.stack(lax.axis_size(("half", "seq")) * [in_array], axis=0), ("half", "seq"), 0, 0
+        ),
+        axis=dim_k,
+    )
+    fragment = map_object_by_axis(0, own_pairs)
     row_max = row_maxima(query_rows, fragment, HD)
     totals, accumulated = weighted_sums(query_rows, fragment, row_max, HD)
     context_rows = (accumulated / totals[:, :, None]).astype(jnp.bfloat16)

time: 442 us -> 461 us (1.043)
  waiting for transfers between devices: 212 us -> 230 us
  starting transfers between devices: 0.26 us -> 7.31 us
    all_to_all x0 -> x1, waiting for transfers between devices: none -> 89.4 us  [on_device(): lax.all_to_all(jnp.stack(lax.axis_size(('half', 'seq')) * [in_array], axi...]
    all_gather x1 -> x0, waiting for transfers between devices: 70.7 us -> none  [on_device(): fragment = lax.all_gather(own_pairs, ('half', 'seq'), axis=0, tiled=True)]
    all_to_all x0 -> x1, starting transfers between devices: none -> 7.28 us  [on_device(): lax.all_to_all(jnp.stack(lax.axis_size(('half', 'seq')) * [in_array], axi...]
    unnamed x15 -> x18, local copies, waits for them, and re-layouts: 13.4 us -> 6.96 us
where the time goes in v1:
time: 461 us; the launch traced here: 459 us
  waiting for transfers between devices  230 us (50%)
  matrix products  125 us (27%)
  local copies, waits for them, and re-layouts  69.8 us (15%)
  between operations  14.2 us (3%)
  other arithmetic  12 us (3%)
  starting transfers between devices  7.31 us (2%)
    reduce_scatter x1, waiting for transfers between devices, on_device(): lax.psum_scatter(pair_grad, ('half', 'seq'), scatter_dimension=0, tiled=T...  140 us
    all_to_all x1, waiting for transfers between devices, on_device(): lax.all_to_all(jnp.stack(lax.axis_size(('half', 'seq')) * [in_array], axi...  89.4 us
    dot_general x24, matrix products, block_scores(): jnp.einsum('rgd,bgd->rgb', query_block, key_rows, preferred_element_type=...  40 us
    dynamic_slice x24, local copies, waits for them, and re-layouts, row_by_rows(): return lax.scan(row_advance, initial, split_blocks(pair_rows))[0]  25.9 us
    dynamic_update_slice x16, local copies, waits for them, and re-layouts, gradients_by_rows(): lax.scan(gradients_advance, jnp.zeros(query_block.shape, jnp.float32), pa...  20.9 us
    dot_general x8, matrix products, gradients_advance(): jnp.einsum('rgb,bgd->rgd', score_grad, key_rows, preferred_element_type=j...  20.5 us
    dot_general x8, matrix products, gradients_advance(): jnp.einsum('rgb,rgd->bgd', probability.astype(jnp.bfloat16), grad_block,...  18.8 us
    dot_general x8, matrix products, gradients_advance(): jnp.einsum('rgd,bgd->rgb', grad_block, values, preferred_element_type=jnp...  18.3 us
  transfers between devices with their start and end apart: 2, of which 2 were waited for; matrix products, arithmetic and copies ran while one was open for 2% of the time, Pallas kernels for 0%

profile of v1, /device:TPU:0, one launch (start us, length us, event | category | flops | bytes accessed | tf_op | source)
XLA Modules:
  0.0 458.7 jit_solution(18422508179417039434)
XLA Ops:
  7.2 5.2 %fusion.23 = f32[1024]{0:T(1024)S(1)} fusion(bf16[1024,4096]{1,0:T(8,128)(2,1)} %param.11), kind=kLoop, calls=%fused_computation.36 | loop fusion | flops 12581888 | bytes 8392704 | tf_op jit(solution)/shard_map/reduce_sum | solution.py:142
  13.6 3.2 fusion.30
  17.0 2.5 stack.8
  19.5 7.3 %all-to-all-start = ((bf16[8,1024,256]{1,2,0:T(8,128)(2,1)}), bf16[8,1024,256]{1,2,0:T(8,128)(2,1)}, u32[]{:S(2)}, u32[]{:S(2)}) async-start(bf16[8,1024,256]{1,2,0:T(8,128)(2,1)} %stack.8), calls=%async_computation | async-start | bytes 8388608 | tf_op jit(solution)/shard_map/all_to_all | solution.py:149
  27.6 1.8 copy.34
  31.5 89.4 %all-to-all-done = bf16[8,1024,256]{1,2,0:T(8,128)(2,1)} async-done(((bf16[8,1024,256]{1,2,0:T(8,128)(2,1)}), bf16[8,1024,256]{1,2,0:T(8,128)(2,1)}, u32[]{:S(2)}, u32[]{:S(2)}) %all-to-all-start) | async-done | bytes 4194336 | tf_op jit(solution)/shard_map/all_to_all | solution.py:149
  120.9 19.5 %while.62 = (s32[]{:T(128)}, f32[1024,2]{0,1:T(2,128)S(1)}, bf16[8,1024,256]{1,2,0:T(8,128)(2,1)}, bf16[1024,2,64]{0,2,1:T(8,128)(2,1)S(1)}, s32[]{:T(128)}, /*index=5*/s32[]{:T(128)}) while((s32[]{:T(128)}, f32[1024,2]{0,1:T(2,128)S(1)}, bf16[8,1024,256]{1,2,0:T(8,128)(2,1)}, bf16[1024,2,64]{0,2,1:T(8,128)(2,1)S(1)}, s32[]{:T(128)}, ...), condition=%wide.region_3.0_spmd.clone, body=%wide.region_1.3_spmd.clone.sunk | while | flops 272631808 | bytes 1605723 | solution.py:56
  140.4 36.4 %while.63 = (s32[]{:T(128)}, f32[1024,2]{0,1:T(2,128)S(1)}, f32[1024,2,64]{0,2,1:T(8,128)S(1)}, bf16[8,1024,256]{1,2,0:T(8,128)(2,1)}, bf16[1024,2,64]{0,2,1:T(8...) while((s32[]{:T(128)}, f32[1024,2]{0,1:T(2,128)S(1)}, ...), condition=%wide.region_6.7_spmd.clone, body=%wide.region_4.0_spmd.clone.sunk | while | flops 549718016 | bytes 19710060 | solution.py:82
  141.5 1.8 fusion.63
  143.3 1.6 fusion.64
  146.1 1.8 fusion.63
  147.9 1.6 fusion.64
  150.6 1.8 fusion.63
  152.4 1.6 fusion.64
  155.2 1.8 fusion.63
  157.0 1.6 fusion.64
  159.7 1.8 fusion.63
  161.5 1.6 fusion.64
  164.2 1.8 fusion.63
  166.0 1.6 fusion.64
  168.8 1.8 fusion.63
  170.6 1.6 fusion.64
  173.3 1.8 fusion.63
  175.1 1.6 fusion.64
  178.3 2.6 multiply_reduce_fusion.1
  181.0 123.8 %while.64 = (s32[]{:T(128)}, f32[1024,2,64]{0,2,1:T(8,128)}, f32[8,1024,256]{2,1,0:T(8,128)}, bf16[8,1024,256]{1,2,0:T(8,128)(2,1)}, bf16[1024,2,64]{0,2,1:T(8,1...) while((s32[]{:T(128)}, f32[1024,2,64]{0,2,1:T(8,128)}, ...), condition=%wide.region_9.10_spmd.clone, body=%wide.region_8.9_spmd.clone.sunk | while | flops 1359478784 | bytes 51142788 | solution.py:122
  182.1 1.9 fusion.72
  184.0 2.3 fusion.75
  186.3 2.3 fusion.73
  188.6 1.6 fusion.74
  192.9 1.6 copy.59
  196.6 1.9 fusion.72
  198.5 2.3 fusion.75
  200.9 2.3 fusion.73
  203.2 2.7 fusion.74
  212.2 1.9 fusion.72
  214.2 2.3 fusion.75
  216.5 2.3 fusion.73
  218.8 2.7 fusion.74
  224.1 1.6 copy.59
  227.8 1.9 fusion.72
  229.8 2.3 fusion.75
  232.1 2.3 fusion.73
  234.4 2.7 fusion.74
  243.4 1.9 fusion.72
  245.4 2.3 fusion.75
  247.7 2.3 fusion.73
  250.0 2.7 fusion.74
  255.3 1.6 copy.59
  259.0 1.9 fusion.72
  260.9 2.3 fusion.75
  263.3 2.3 fusion.73
  265.6 2.7 fusion.74
  274.6 1.9 fusion.72
  276.6 2.3 fusion.75
  278.9 2.3 fusion.73
  281.2 2.7 fusion.74
  286.5 1.6 copy.59
  290.3 1.9 fusion.72
  292.2 2.3 fusion.75
  294.5 2.3 fusion.73
  296.8 2.7 fusion.74
  309.6 140.2 %reduce-scatter.2.cloned.1.call-done = f32[1024,256]{1,0:T(8,128)} async-done(((f32[8192,256]{1,0:T(8,128)}), f32[1024,256]{1,0:T(8,128)}) %reduce-scatter.2.cloned.1.call-update) | async-done | bytes 1048592 | tf_op jit(solution)/shard_map/reduce_scatter | solution.py:160
  449.8 2.1 convert_element_type.49
  (119 shorter events, 83.1 us)
Async XLA Ops:
  7.2 5.3 %copy-start = (bf16[4096,256]{1,0:T(8,128)(2,1)S(1)}, bf16[4096,256]{1,0:T(8,128)(2,1)}, u32[]{:S(2)}) copy-start(bf16[4096,256]{1,0:T(8,128)(2,1)} %param.13) | copy-start | bytes 6291460
  7.2 6.4 %copy-start.1 = (bf16[1024,4096]{1,0:T(8,128)(2,1)S(1)}, bf16[1024,4096]{1,0:T(8,128)(2,1)}, u32[]{:S(2)}) copy-start(bf16[1024,4096]{1,0:T(8,128)(2,1)} %param.11) | copy-start | bytes 25165828
  17.0 9.9 %copy-start.5 = (bf16[128,1024]{1,0:T(8,128)(2,1)S(1)}, bf16[128,1024]{1,0:T(8,128)(2,1)}, u32[]{:S(2)}) copy-start(bf16[128,1024]{1,0:T(8,128)(2,1)} %param.14) | copy-start | bytes 786436
  19.5 101.4 %all-to-all-start = ((bf16[8,1024,256]{1,2,0:T(8,128)(2,1)}), bf16[8,1024,256]{1,2,0:T(8,128)(2,1)}, u32[]{:S(2)}, u32[]{:S(2)}) async-start(bf16[8,1024,256]{1,2,0:T(8,128)(2,1)} %stack.8), calls=%async_computation | async-start | bytes 8388608 | tf_op jit(solution)/shard_map/all_to_all | solution.py:149
  26.8 423.0 %reduce-scatter.2.cloned.1.call-start = ((), (), s32[]{:S(2)}) async-start(), calls=%async_computation.2 | async-start | bytes 9437184 | tf_op jit(solution)/shard_map/reduce_scatter | solution.py:160
  30.6 90.3 %copy-start.2 = (bf16[128,2,8,64]{3,2,0,1:T(8,128)(2,1)}, bf16[128,2,8,64]{3,2,0,1:T(8,128)(2,1)S(1)}, u32[]{:S(2)}) copy-start(bf16[128,2,8,64]{3,2,0,1:T(8,128)(2,1)S(1)} %copy.35) | copy-start | bytes 786436
  140.4 37.9 %copy-start.3 = (bf16[128,2,8,64]{3,2,0,1:T(8,128)(2,1)S(1)}, bf16[128,2,8,64]{3,2,0,1:T(8,128)(2,1)}, u32[]{:S(2)}) copy-start(bf16[128,2,8,64]{3,2,0,1:T(8,128)(2,1)} %copy-done.2) | copy-start | bytes 786436
  304.8 1.0 copy-start.4
Sparse Core Ops, SparseCore 0:
  304.9 144.8 reduce-scatter.1
